TPU v7x, 256 devices: a whole 4x4x8 slice. The times are simulated.
256 devices in a mesh: crop: 2 (over y_hi), rows: 16 (over y_lo, x, core), hid: 8 (over z).
Axes of the slice: x: 4, y: 4 (y_hi: 2, y_lo: 2; y = y_hi * 2 + y_lo), z: 8, core: 2. Of those that a mesh axis runs over, the one named last changes fastest.
Arguments:
- tokens: bfloat16 [2, 32, 64, 4096], P('crop', 'rows', None, 'hid'), may hold values from -6 to 6
- cotangent: bfloat16 [2, 32, 64, 4096], P('crop', 'rows', None, 'hid'), may hold values from -6 to 6
- weight_in: bfloat16 [256, 64, 5, 256], P('rows', 'hid'), may hold values from -0.15625 to 0.15625
- weight_out: bfloat16 [256, 64, 5, 256], P('rows', 'hid'), may hold values from -0.078125 to 0.078125
- mix_kernel: float32 [9, 16384], P(None, 'hid'), may hold values from -4 to 4
- block_rows: int32 [64, 5], P('hid'), may hold values from 0 to 15, as said below
Outputs:
- grad_tokens: bfloat16 [2, 32, 64, 4096], P('crop', 'rows', None, 'hid')
- grad_w_in: float32 [256, 64, 5, 256], P(('crop', 'rows'), 'hid')
- grad_w_out: float32 [256, 64, 5, 256], P(('crop', 'rows'), 'hid')
- grad_kernel: float32 [9, 16384], P(None, 'hid')
Inputs may be any that keep to these rules, and one draw needn't show every extreme that they name: In each block column c, block_rows[c, 0] is a label L and block_rows[c, k] for k >= 1 is L with bit k - 1 flipped, so the 5 entries of a column differ; every value is the label of equally many block columns.
All inputs are finite; a program needn't handle non-finite values.
Results may differ from a plain program's by a relative error of at most 0.019.
Values may be sent and summed in bfloat16 or wider, within the bound.
No kernel may reach another device: no remote copies, remote signals or barrier semaphores. Data moves between devices by JAX's collectives and lax.ppermute only.
A program may use at most 128 MiB of HBM per device.

v0:
```python
import jax
import jax.numpy as jnp
from jax import lax
from jax.sharding import PartitionSpec as P

root_two_pi = 0.7978845608
cubic_coef = 0.044715
loss_scale = 0.03125


def padded(shard, sides, width):
    for axis, dim in sides:
        devices, length = (lax.axis_size(axis), shard.shape[dim])
        up = [(i, (i + 1) % devices) for i in range(devices - 1)]
        down = [(j, i) for i, j in up]
        last = lax.slice_in_dim(shard, length - width, length, axis=dim)
        initial = lax.slice_in_dim(shard, 0, width, axis=dim)
        before = lax.ppermute(last, axis, up)
        after = lax.ppermute(initial, axis, down)
        shard = jnp.concatenate([before, shard, after], axis=dim)
    return shard


def gelu_pair(preact):
    inner = root_two_pi * (preact + cubic_coef * preact * preact * preact)
    tanh_val = jnp.tanh(inner)
    gelu_out = 0.5 * preact * (1.0 + tanh_val)
    slopes = 0.5 * (1.0 + tanh_val) + 0.5 * preact * (1.0 - tanh_val * tanh_val) * root_two_pi * (
        1.0 + 3.0 * cubic_coef * preact * preact
    )
    return (gelu_out, slopes)


def on_device(tokens, cotangent, weight_in, weight_out, mix_kernel, block_rows):
    in_panel, out_panel = (
        lax.all_gather(weight_in, "rows", axis=0, tiled=True),
        lax.all_gather(weight_out, "rows", axis=0, tiled=True),
    )
    tok_full, cot_full = (
        lax.all_gather(tokens, "hid", axis=3, tiled=True),
        lax.all_gather(cotangent, "hid", axis=3, tiled=True),
    )
    crop_count, height, grid_width, depth_all = tok_full.shape
    tok_count = crop_count * height * grid_width
    block_size = in_panel.shape[0]
    col_count = in_panel.shape[1]
    nnz_count = in_panel.shape[2]
    block_count = depth_all // block_size
    hidden_local = col_count * block_size
    flat_rows = block_rows.reshape(-1)
    in_select = jnp.take(
        tok_full.reshape(tok_count, block_count, block_size), flat_rows, axis=1
    ).reshape(tok_count, col_count, nnz_count, block_size)
    grad_select = jnp.take(
        cot_full.reshape(tok_count, block_count, block_size), flat_rows, axis=1
    ).reshape(tok_count, col_count, nnz_count, block_size)
    pre_act = jnp.einsum("tckb,bcke->tce", in_select, in_panel, preferred_element_type=jnp.float32)
    gelu_out, slopes = gelu_pair(pre_act)
    active = gelu_out.astype(jnp.bfloat16).reshape(crop_count, height, grid_width, hidden_local)
    act_rim = padded(active, (("rows", 1),), 1)
    mix_grad = (
        jnp.einsum("tckd,fckd->tcf", grad_select, out_panel, preferred_element_type=jnp.float32)
        .astype(jnp.bfloat16)
        .reshape(crop_count, height, grid_width, hidden_local)
    )
    grad_rim = padded(mix_grad, (("rows", 1),), 1)
    act_pad = jnp.pad(act_rim.astype(jnp.float32), ((0, 0), (0, 0), (1, 1), (0, 0)))
    grad_pad = jnp.pad(grad_rim.astype(jnp.float32), ((0, 0), (0, 0), (1, 1), (0, 0)))
    grad_grid = mix_grad.astype(jnp.float32)
    mix_sum = jnp.zeros((crop_count, height, grid_width, hidden_local), jnp.float32)
    act_grad = jnp.zeros((crop_count, height, grid_width, hidden_local), jnp.float32)
    kern_terms = []
    for row_off in range(3):
        for col_off in range(3):
            tap = mix_kernel[3 * row_off + col_off]
            shifted = act_pad[:, row_off : row_off + height, col_off : col_off + grid_width]
            mix_sum = mix_sum + tap * shifted
            act_grad = (
                act_grad
                + tap
                * grad_pad[
                    :, 2 - row_off : 2 - row_off + height, 2 - col_off : 2 - col_off + grid_width
                ]
            )
            kern_terms.append(jnp.sum(shifted * grad_grid, axis=(0, 1, 2)))
    kern_local = jnp.stack(kern_terms, axis=0) * loss_scale
    mix_out = mix_sum.astype(jnp.bfloat16).reshape(tok_count, col_count, block_size)
    pre_grad = (act_grad.reshape(tok_count, col_count, block_size) * slopes).astype(jnp.bfloat16)
    kern_total = lax.psum(kern_local.astype(jnp.bfloat16), ("crop", "rows")).astype(jnp.float32)
    back_select = jnp.einsum(
        "tce,bcke->tckb", pre_grad, in_panel, preferred_element_type=jnp.float32
    )
    one_hot = (
        block_rows[:, :, None] == jnp.arange(block_count, dtype=jnp.int32)[None, None, :]
    ).astype(jnp.float32)
    token_terms = jnp.einsum(
        "tckb,ckr->trb", back_select, one_hot, precision=lax.Precision.HIGHEST
    ).reshape(crop_count, height, grid_width, depth_all)
    grad_tokens = lax.psum_scatter(
        token_terms.astype(jnp.bfloat16), "hid", scatter_dimension=3, tiled=True
    )
    first_term = jnp.einsum(
        "tckb,tce->bcke", in_select, pre_grad, preferred_element_type=jnp.float32
    )
    second_term = jnp.einsum(
        "tcf,tckd->fckd", mix_out, grad_select, preferred_element_type=jnp.float32
    )
    share_sums = lax.psum_scatter(
        (jnp.stack([first_term, second_term], axis=1) * loss_scale).astype(jnp.bfloat16),
        ("crop", "rows"),
        scatter_dimension=0,
        tiled=True,
    ).astype(jnp.float32)
    return (grad_tokens, share_sums[:, 0], share_sums[:, 1], kern_total)


def solution(mesh):
    placed = (
        P("crop", "rows", None, "hid"),
        P("crop", "rows", None, "hid"),
        P("rows", "hid", None, None),
        P("rows", "hid", None, None),
        P(None, "hid"),
        P("hid", None),
    )
    return jax.shard_map(
        on_device,
        mesh=mesh,
        in_specs=placed,
        out_specs=(
            P("crop", "rows", None, "hid"),
            P(("crop", "rows"), "hid", None, None),
            P(("crop", "rows"), "hid", None, None),
            P(None, "hid"),
        ),
        check_vma=False,
    )
```

profile of v0, /device:TPU:4, one launch (start us, length us, event | category | flops | bytes accessed | tf_op | source)
XLA Modules:
  0.0 380.4 jit_solution(11429003799002727429)
XLA Ops:
  13.2 38.3 %all-gather.9.cloned.1.call-done = bf16[1,2,64,4096]{3,2,1,0:T(8,128)(2,1)} async-done(((bf16[1,2,64,512]{3,2,1,0:T(8,128)(2,1)}), bf16[1,2,64,4096]{3,2,1,0:T(8,128)(2,1)}) %all-gather.9.cloned.1.call-update) | async-done | bytes 1048592 | tf_op jit(solution)/shard_map/all_gather | solution.py:40
  53.3 37.1 %all-gather.5.cloned.1.call-done = bf16[1,2,64,4096]{3,2,1,0:T(8,128)(2,1)} async-done(((bf16[1,2,64,512]{3,2,1,0:T(8,128)(2,1)}), bf16[1,2,64,4096]{3,2,1,0:T(8,128)(2,1)}) %all-gather.5.cloned.1.call-update) | async-done | bytes 1048592 | tf_op jit(solution)/shard_map/all_gather | solution.py:41
  92.2 2.4 gather_fusion.1
  94.6 2.4 gather_fusion
  97.0 4.6 %broadcast_select_fusion.1 = (bf16[40,128,256]{2,1,0:T(8,128)(2,1)S(1)}, bf16[40,128,256]{2,1,0:T(8,128)(2,1)}) fusion(bf16[40,128,256]{2,1,0:T(8,128)(2,1)} %gather_fusion, pred[40]{0:T(512)(128)(4,1)S(1)} %compare_and_fusion, bf16[40,128,256]{2,1,0:T(8,128)(2,1)} %gather_fusion.1), kind=kLoop, calls=%fused_computation.18 | loop fusion | flops 2621440 | bytes 10485800 | tf_op jit(solution)/shard_map/jit(_take)/select_n | solution.py:54
  101.6 30.2 %all-gather.7.cloned.1.call-done = bf16[256,8,5,256]{3,0,2,1:T(8,128)(2,1)} async-done(((bf16[16,8,5,256]{3,0,2,1:T(8,128)(2,1)}), bf16[256,8,5,256]{3,0,2,1:T(8,128)(2,1)}) %all-gather.7.cloned.1.call-update) | async-done | bytes 5242896 | tf_op jit(solution)/shard_map/all_gather | solution.py:37
  131.8 4.3 %fusion.9 = bf16[128,8,256]{2,0,1:T(8,128)(2,1)S(1)} fusion(bf16[128,8,5,256]{3,0,2,1:T(8,128)(2,1)S(1)} %bitcast.97, bf16[256,8,5,256]{3,0,2,1:T(8,128)(2,1)} %all-gather.7.cloned.1.call-done), kind=kOutput, calls=%fused_computation.39 | convolution fusion | flops 671350784 | bytes 8388608 | tf_op jit(solution)/shard_map/tckd,fckd->tcf/dot_general | solution.py:62
  138.6 2.1 collective-permute-start
  140.7 3.4 collective-permute-start.1
  144.2 2.0 collective-permute-done
  146.3 3.6 collective-permute-done.1
  152.2 25.9 %all-gather.11.cloned.1.call-done = bf16[256,8,5,256]{3,0,2,1:T(8,128)(2,1)} async-done(((bf16[16,8,5,256]{3,0,2,1:T(8,128)(2,1)}), bf16[256,8,5,256]{3,0,2,1:T(8,128)(2,1)}) %all-gather.11.cloned.1.call-update) | async-done | bytes 5242896 | tf_op jit(solution)/shard_map/all_gather | solution.py:36
  178.1 5.1 %multiply_convert_fusion = (bf16[128,8,256]{2,0,1:T(8,128)(2,1)S(1)}, bf16[128,8,256]{2,0,1:T(8,128)(2,1)}) fusion(f32[128,8,256]{2,1,0:T(8,128)} %bitcast.108, bf16[128,8,5,256]{3,0,2,1:T(8,128)(2,1)S(1)} %bitcast.99, bf16[256,8,5,256]{3,0,2,1:T(8,128)(2,1)} %all-gather.11.cloned.1.call-done), kind=kOutput, calls=%fused_computation.76 | convolution fusion | flops 676593664 | bytes 9961472 | tf_op jit(solution)/shard_map/tckb,bcke->tce/dot_general | solution.py:57
  184.4 2.1 reshape.189
  187.5 2.1 collective-permute-start.2
  189.7 3.6 collective-permute-start.3
  193.3 2.7 convolution_bitcast_fusion.1
  200.5 5.7 %fusion = bf16[256,2,8,5,256]{0,4,3,2,1:T(8,128)(2,1)} fusion(f32[256,1,8,5,256]{0,4,3,2,1:T(8,128)S(1)} %convolution_bitcast_fusion, f32[256,1,8,5,256]{0,4,3,2,1:T(8,128)S(1)} %convolution_bitcast_fusion.1), kind=kLoop, calls=%fused_computation.3 | loop fusion | flops 15728640 | bytes 31457280 | tf_op jit(solution)/shard_map/convert_element_type | solution.py:109
  206.2 15.4 %copy.56 = bf16[256,2,8,5,256]{4,2,3,1,0:T(8,128)(2,1)} copy(bf16[256,2,8,5,256]{0,4,3,2,1:T(8,128)(2,1)} %fusion) | data formatting | bytes 20971520 | tf_op jit(solution)/shard_map/convert_element_type | solution.py:109
  222.6 4.3 %convolution_bitcast_fusion.2 = f32[128,8,5,256]{3,0,2,1:T(8,128)S(1)} fusion(bf16[256,8,5,256]{3,0,2,1:T(8,128)(2,1)} %all-gather.11.cloned.1.call-done, bf16[128,8,256]{2,0,1:T(8,128)(2,1)S(1)} %copy-done.4), kind=kOutput, calls=%fused_computation.19 | convolution fusion | flops 671088640 | bytes 11010048 | tf_op jit(solution)/shard_map/tce,bcke->tckb/dot_general | solution.py:90
  227.0 5.9 %fusion.5 = bf16[128,16,256]{2,1,0:T(8,128)(2,1)} fusion(f32[128,8,5,256]{3,0,2,1:T(8,128)S(1)} %convolution_bitcast_fusion.2, s32[8,5]{0,1:T(8,128)S(1)} %copy.44), kind=kOutput, calls=%fused_computation.35 | convolution fusion | flops 252183168 | bytes 6291616 | tf_op jit(solution)/shard_map/tckb,ckr->trb/dot_general | solution.py:96
  232.8 2.3 convert_element_type.87
  236.4 117.1 %psum.7 = bf16[9,2048]{1,0:T(8,128)(2,1)S(1)} all-reduce(bf16[9,2048]{1,0:T(8,128)(2,1)S(1)} %multiply_convert_fusion.1), channel_id=1, replica_groups=mesh['crop'=2,'rows'=16,'hid'=8] {'crop','rows'}, use_global_device_ids=true, to_apply=%region_11.13 | all-reduce | flops 18432 | bytes 73728 | tf_op jit(solution)/shard_map/psum | solution.py:89
  356.1 17.5 %reduce-scatter.3.cloned.1.call-done = bf16[1,2,64,512]{3,2,1,0:T(8,128)(2,1)} async-done(((bf16[1,2,64,4096]{3,2,1,0:T(8,128)(2,1)}), bf16[1,2,64,512]{3,2,1,0:T(8,128)(2,1)}) %reduce-scatter.3.cloned.1.call-update) | async-done | bytes 131088 | tf_op jit(solution)/shard_map/reduce_scatter | solution.py:99
  (59 shorter events, 25.8 us)
Async XLA Ops:
  7.2 44.3 %all-gather.9.cloned.1.call-start = ((), (), s32[]{:S(2)}) async-start(), calls=%async_computation.4 | async-start | bytes 1179648 | tf_op jit(solution)/shard_map/all_gather | solution.py:40
  7.9 82.5 %all-gather.5.cloned.1.call-start = ((), (), s32[]{:S(2)}) async-start(), calls=%async_computation.2 | async-start | bytes 1179648 | tf_op jit(solution)/shard_map/all_gather | solution.py:41
  8.6 123.2 %all-gather.7.cloned.1.call-start = ((), (), s32[]{:S(2)}) async-start(), calls=%async_computation.3 | async-start | bytes 5570560 | tf_op jit(solution)/shard_map/all_gather | solution.py:37
  10.5 167.7 %all-gather.11.cloned.1.call-start = ((), (), s32[]{:S(2)}) async-start(), calls=%async_computation.5 | async-start | bytes 5570560 | tf_op jit(solution)/shard_map/all_gather | solution.py:36
  12.3 341.8 %reduce-scatter.5.cloned.1.call-start = ((), (), s32[]{:S(2)}) async-start(), calls=%async_computation.7 | async-start | bytes 10813440 | tf_op jit(solution)/shard_map/reduce_scatter | solution.py:108
  101.6 34.5 %copy-start = (bf16[40,128,256]{2,1,0:T(8,128)(2,1)}, bf16[40,128,256]{2,1,0:T(8,128)(2,1)S(1)}, u32[]{:S(2)}) copy-start(bf16[40,128,256]{2,1,0:T(8,128)(2,1)S(1)} %get-tuple-element.43) | copy-start | bytes 7864324
  136.1 8.0 %copy-start.5 = (f32[9,2048]{1,0:T(8,128)S(1)}, f32[9,2048]{1,0:T(8,128)}, u32[]{:S(2)}) copy-start(f32[9,2048]{1,0:T(8,128)} %param.12) | copy-start | bytes 221188
  138.6 7.7 %collective-permute-start = (bf16[1,1,64,2048]{3,2,1,0:T(8,128)(2,1)S(1)}, bf16[1,1,64,2048]{3,2,1,0:T(8,128)(2,1)S(1)}, u32[]{:S(2)}, u32[]{:S(2)}) collective-permute-start(bf16[1,1,64,2048]{3,2,1,0:T(8,128)(2,1)S(1)} %get-tuple-element.32), channel_id=1, source_target_pairs={{0,8},{8,16},{16,24},{24,32},{32,40},{40,48},{48,56},{56,64},{64,7... | collective-permute-start | bytes 786440 | tf_op jit(solution)/shard_map/ppermute | solution.py:18
  140.7 9.2 %collective-permute-start.1 = (bf16[1,1,64,2048]{3,2,1,0:T(8,128)(2,1)S(1)}, bf16[1,1,64,2048]{3,2,1,0:T(8,128)(2,1)S(1)}, u32[]{:S(2)}, u32[]{:S(2)}) collective-permute-start(bf16[1,1,64,2048]{3,2,1,0:T(8,128)(2,1)S(1)} %get-tuple-element.33), channel_id=1, source_target_pairs={{8,0},{16,8},{24,16},{32,24},{40,32},{48,40},{56,48},{64,56},{72,6... | collective-permute-start | bytes 786440 | tf_op jit(solution)/shard_map/ppermute | solution.py:19
  150.0 28.1 %copy-start.2 = (bf16[40,128,256]{2,1,0:T(8,128)(2,1)S(1)}, bf16[40,128,256]{2,1,0:T(8,128)(2,1)}, u32[]{:S(2)}) copy-start(bf16[40,128,256]{2,1,0:T(8,128)(2,1)} %get-tuple-element.44) | copy-start | bytes 7864324
  187.5 8.4 %collective-permute-start.2 = (bf16[1,1,64,2048]{3,2,1,0:T(8,128)(2,1)S(1)}, bf16[1,1,64,2048]{3,2,1,0:T(8,128)(2,1)S(1)}, u32[]{:S(2)}, u32[]{:S(2)}) collective-permute-start(bf16[1,1,64,2048]{3,2,1,0:T(8,128)(2,1)S(1)} %get-tuple-element.30), channel_id=1, source_target_pairs={{0,8},{8,16},{16,24},{24,32},{32,40},{40,48},{48,56},{56,64},{64,7... | collective-permute-start | bytes 786440 | tf_op jit(solution)/shard_map/ppermute | solution.py:18
  189.7 7.3 %collective-permute-start.3 = (bf16[1,1,64,2048]{3,2,1,0:T(8,128)(2,1)S(1)}, bf16[1,1,64,2048]{3,2,1,0:T(8,128)(2,1)S(1)}, u32[]{:S(2)}, u32[]{:S(2)}) collective-permute-start(bf16[1,1,64,2048]{3,2,1,0:T(8,128)(2,1)S(1)} %get-tuple-element.31), channel_id=1, source_target_pairs={{8,0},{16,8},{24,16},{32,24},{40,32},{48,40},{56,48},{64,56},{72,6... | collective-permute-start | bytes 786440 | tf_op jit(solution)/shard_map/ppermute | solution.py:19
  193.3 3.7 copy-start.3
  197.2 1.7 copy-start.1
  221.6 0.7 copy-start.6
  221.6 1.1 copy-start.4
  221.6 152.0 %reduce-scatter.3.cloned.1.call-start = ((), (), s32[]{:S(2)}) async-start(), calls=%async_computation.6 | async-start | bytes 1179648 | tf_op jit(solution)/shard_map/reduce_scatter | solution.py:99
Sparse Core Ops, SparseCore 0:
  9.8 41.6 all-gather.8
  53.3 37.0 all-gather.4
  92.8 39.0 all-gather.6
  134.0 44.0 all-gather.10
  221.7 110.2 reduce-scatter.4
  335.1 38.3 reduce-scatter.2
where the time goes:
time: 381 us; the launch traced here: 380 us
  waiting for transfers between devices  157 us (41%)
  blocking collectives  117 us (31%)
  local copies, waits for them, and re-layouts  41.1 us (11%)
  matrix products  23.8 us (6%)
  other arithmetic  15.2 us (4%)
  between operations  14.3 us (4%)
  starting transfers between devices  11.8 us (3%)
    psum x1, blocking collectives, on_device(): lax.psum(kern_local.astype(jnp.bfloat16), ('crop', 'rows'))  117 us
    all_gather x1, waiting for transfers between devices, on_device(): lax.all_gather(tokens, 'hid', axis=3, tiled=True)  38.3 us
    all_gather x1, waiting for transfers between devices, on_device(): lax.all_gather(cotangent, 'hid', axis=3, tiled=True)  37.1 us
    all_gather x1, waiting for transfers between devices, on_device(): lax.all_gather(weight_out, 'rows', axis=0, tiled=True)  30.2 us
    all_gather x1, waiting for transfers between devices, on_device(): lax.all_gather(weight_in, 'rows', axis=0, tiled=True)  25.9 us
    reduce_scatter x1, waiting for transfers between devices, on_device(): lax.psum_scatter(token_terms.astype(jnp.bfloat16), 'hid', scatter_dimensi...  17.5 us
    convert_element_type x1, local copies, waits for them, and re-layouts, on_device(): (jnp.stack([first_term, second_term], axis=1) * loss_scale).astype(jnp.bf...  15.4 us
    unnamed x21, local copies, waits for them, and re-layouts  9.42 us
  transfers between devices with their start and end apart: 10, of which 8 were waited for; matrix products, arithmetic and copies ran while one was open for 12% of the time, Pallas kernels for 0%

commit v1 on v0

--- a/solution.py
+++ b/solution.py
@@ -6,6 +6,27 @@
 root_two_pi = 0.7978845608
 cubic_coef = 0.044715
 loss_scale = 0.03125
+
+
+def ring_gather(array, axis, dim):
+    devices, here, rows = (lax.axis_size(axis), lax.axis_index(axis), array.shape[dim])
+    upward = [(i, (i + 1) % devices) for i in range(devices)]
+    downward = [(i, (i - 1) % devices) for i in range(devices)]
+    result = jnp.zeros((*array.shape[:dim], devices * rows, *array.shape[dim + 1 :]), array.dtype)
+    result = lax.dynamic_update_slice_in_dim(result, array, here * rows, axis=dim)
+    from_left = from_right = array
+    halfway = devices // 2
+    for lap in range(1, halfway + 1):
+        from_left = lax.ppermute(from_left, axis, upward)
+        result = lax.dynamic_update_slice_in_dim(
+            result, from_left, (here - lap) % devices * rows, axis=dim
+        )
+        if lap < devices - halfway:
+            from_right = lax.ppermute(from_right, axis, downward)
+            result = lax.dynamic_update_slice_in_dim(
+                result, from_right, (here + lap) % devices * rows, axis=dim
+            )
+    return result
 
 
 def padded(shard, sides, width):
@@ -37,7 +58,7 @@
         lax.all_gather(weight_out, "rows", axis=0, tiled=True),
     )
     tok_full, cot_full = (
-        lax.all_gather(tokens, "hid", axis=3, tiled=True),
+        ring_gather(tokens, "hid", 3),
         lax.all_gather(cotangent, "hid", axis=3, tiled=True),
     )
     crop_count, height, grid_width, depth_all = tok_full.shape

time: 381 us -> 343 us (0.900)
  waiting for transfers between devices: 157 us -> 107 us
  starting transfers between devices: 11.8 us -> 24.9 us
    all_gather x1 -> x0, waiting for transfers between devices: 38.3 us -> none  [on_device(): lax.all_gather(tokens, 'hid', axis=3, tiled=True)]
    all_gather x1, waiting for transfers between devices: 37.1 us -> 3.63 us  [on_device(): lax.all_gather(cotangent, 'hid', axis=3, tiled=True)]
    ppermute x0 -> x7, waiting for transfers between devices: none -> 19.7 us  [the longest x4 14.4 us: ring_gather(): from_left = lax.ppermute(from_left, axis, upward)]
    ppermute x0 -> x7, starting transfers between devices: none -> 13.2 us  [the longest x3 13.2 us: ring_gather(): from_right = lax.ppermute(from_right, axis, downward)]
    unnamed x21 -> x23, local copies, waits for them, and re-layouts: 9.42 us -> 8.19 us
  transfers between devices with their start and end apart: 10 -> 16, of which waited for: 8 -> 11; matrix products, arithmetic and copies ran while one was open for 12% -> 13% of each run, Pallas kernels for 0% -> 0%
where the time goes in v1:
time: 343 us; the launch traced here: 342 us
  blocking collectives  117 us (34%)
  waiting for transfers between devices  107 us (31%)
  local copies, waits for them, and re-layouts  40 us (12%)
  starting transfers between devices  24.9 us (7%)
  matrix products  23.8 us (7%)
  other arithmetic  15.1 us (4%)
  between operations  14.2 us (4%)
    psum x1, blocking collectives, on_device(): lax.psum(kern_local.astype(jnp.bfloat16), ('crop', 'rows'))  117 us
    all_gather x1, waiting for transfers between devices, on_device(): lax.all_gather(weight_out, 'rows', axis=0, tiled=True)  32.3 us
    all_gather x1, waiting for transfers between devices, on_device(): lax.all_gather(weight_in, 'rows', axis=0, tiled=True)  26.4 us
    reduce_scatter x1, waiting for transfers between devices, on_device(): lax.psum_scatter(token_terms.astype(jnp.bfloat16), 'hid', scatter_dimensi...  17.4 us
    convert_element_type x1, local copies, waits for them, and re-layouts, on_device(): (jnp.stack([first_term, second_term], axis=1) * loss_scale).astype(jnp.bf...  15.4 us
    ppermute x4, waiting for transfers between devices, ring_gather(): from_left = lax.ppermute(from_left, axis, upward)  14.4 us
    ppermute x3, starting transfers between devices, ring_gather(): from_right = lax.ppermute(from_right, axis, downward)  13.2 us
    unnamed x23, local copies, waits for them, and re-layouts  8.19 us
  transfers between devices with their start and end apart: 16, of which 11 were waited for; matrix products, arithmetic and copies ran while one was open for 13% of the time, Pallas kernels for 0%

profile of v1, /device:TPU:4, one launch (start us, length us, event | category | flops | bytes accessed | tf_op | source)
XLA Modules:
  0.0 341.8 jit_solution(3259652234687622958)
XLA Ops:
  11.6 5.9 %collective-permute-start.3 = (bf16[1,2,64,512]{3,2,1,0:T(8,128)(2,1)}, bf16[1,2,64,512]{3,2,1,0:T(8,128)(2,1)S(1)}, u32[]{:S(2)}, u32[]{:S(2)}) collective-permute-start(bf16[1,2,64,512]{3,2,1,0:T(8,128)(2,1)} %param.8), channel_id=1, source_target_pairs={{0,7},{1,0},{2,1},{3,2},{4,3},{5,4},{6,5},{7,6},{8,15},{9,8},{10,9... | collective-permute-start | bytes 393224 | tf_op jit(solution)/shard_map/ppermute | solution.py:25
  20.6 3.6 %collective-permute-start.5 = (bf16[1,2,64,512]{3,2,1,0:T(8,128)(2,1)S(1)}, bf16[1,2,64,512]{3,2,1,0:T(8,128)(2,1)S(1)}, u32[]{:S(2)}, u32[]{:S(2)}) collective-permute-start(bf16[1,2,64,512]{3,2,1,0:T(8,128)(2,1)S(1)} %collective-permute-done.3), channel_id=1, source_target_pairs={{0,7},{1,0},{2,1},{3,2},{4,3},{5,4},{6,5},{7,6},{8,15},{9,8},{10,9... | collective-permute-start | bytes 393224 | tf_op jit(solution)/shard_map/ppermute | solution.py:25
  24.3 3.2 collective-permute-done.5
  27.5 3.7 %collective-permute-start.7 = (bf16[1,2,64,512]{3,2,1,0:T(8,128)(2,1)S(1)}, bf16[1,2,64,512]{3,2,1,0:T(8,128)(2,1)S(1)}, u32[]{:S(2)}, u32[]{:S(2)}) collective-permute-start(bf16[1,2,64,512]{3,2,1,0:T(8,128)(2,1)S(1)} %collective-permute-done.5), channel_id=1, source_target_pairs={{0,7},{1,0},{2,1},{3,2},{4,3},{5,4},{6,5},{7,6},{8,15},{9,8},{10,9... | collective-permute-start | bytes 393224 | tf_op jit(solution)/shard_map/ppermute | solution.py:25
  31.2 7.2 %collective-permute-done.6 = bf16[1,2,64,512]{3,2,1,0:T(8,128)(2,1)S(1)} collective-permute-done((bf16[1,2,64,512]{3,2,1,0:T(8,128)(2,1)S(1)}, bf16[1,2,64,512]{3,2,1,0:T(8,128)(2,1)S(1)}, u32[]{:S(2)}, u32[]{:S(2)}) %collective-permute-start.6) | collective-permute-done | bytes 131104 | tf_op jit(solution)/shard_map/ppermute | solution.py:20
  38.5 7.2 %collective-permute-done.8 = bf16[1,2,64,512]{3,2,1,0:T(8,128)(2,1)S(1)} collective-permute-done((bf16[1,2,64,512]{3,2,1,0:T(8,128)(2,1)S(1)}, bf16[1,2,64,512]{3,2,1,0:T(8,128)(2,1)S(1)}, u32[]{:S(2)}, u32[]{:S(2)}) %collective-permute-start.8) | collective-permute-done | bytes 131104 | tf_op jit(solution)/shard_map/ppermute | solution.py:20
  46.3 2.4 gather_fusion.1
  48.7 3.6 %all-gather.4.cloned.1.call-done = bf16[1,2,64,4096]{3,2,1,0:T(8,128)(2,1)} async-done(((bf16[1,2,64,512]{3,2,1,0:T(8,128)(2,1)}), bf16[1,2,64,4096]{3,2,1,0:T(8,128)(2,1)}) %all-gather.4.cloned.1.call-update) | async-done | bytes 1048592 | tf_op jit(solution)/shard_map/all_gather | solution.py:62
  54.1 2.4 gather_fusion
  56.6 4.6 %broadcast_select_fusion.1 = (bf16[40,128,256]{2,1,0:T(8,128)(2,1)S(1)}, bf16[40,128,256]{2,1,0:T(8,128)(2,1)}) fusion(bf16[40,128,256]{2,1,0:T(8,128)(2,1)} %gather_fusion, pred[40]{0:T(512)(128)(4,1)S(1)} %compare_and_fusion, bf16[40,128,256]{2,1,0:T(8,128)(2,1)} %gather_fusion.1), kind=kLoop, calls=%fused_computation.18 | loop fusion | flops 2621440 | bytes 10485800 | tf_op jit(solution)/shard_map/jit(_take)/select_n | solution.py:75
  61.2 32.3 %all-gather.6.cloned.1.call-done = bf16[256,8,5,256]{3,0,2,1:T(8,128)(2,1)} async-done(((bf16[16,8,5,256]{3,0,2,1:T(8,128)(2,1)}), bf16[256,8,5,256]{3,0,2,1:T(8,128)(2,1)}) %all-gather.6.cloned.1.call-update) | async-done | bytes 5242896 | tf_op jit(solution)/shard_map/all_gather | solution.py:58
  93.5 4.3 %fusion.9 = bf16[128,8,256]{2,0,1:T(8,128)(2,1)S(1)} fusion(bf16[128,8,5,256]{3,0,2,1:T(8,128)(2,1)S(1)} %bitcast.97, bf16[256,8,5,256]{3,0,2,1:T(8,128)(2,1)} %all-gather.6.cloned.1.call-done), kind=kOutput, calls=%fused_computation.39 | convolution fusion | flops 671350784 | bytes 8388608 | tf_op jit(solution)/shard_map/tckd,fckd->tcf/dot_general | solution.py:83
  102.4 3.6 %collective-permute-start.1 = (bf16[1,1,64,2048]{3,2,1,0:T(8,128)(2,1)S(1)}, bf16[1,1,64,2048]{3,2,1,0:T(8,128)(2,1)S(1)}, u32[]{:S(2)}, u32[]{:S(2)}) collective-permute-start(bf16[1,1,64,2048]{3,2,1,0:T(8,128)(2,1)S(1)} %get-tuple-element.33), channel_id=1, source_target_pairs={{8,0},{16,8},{24,16},{32,24},{40,32},{48,40},{56,48},{64,56},{72,6... | collective-permute-start | bytes 786440 | tf_op jit(solution)/shard_map/ppermute | solution.py:40
  107.9 3.3 collective-permute-done.1
  113.6 26.4 %all-gather.8.cloned.1.call-done = bf16[256,8,5,256]{3,0,2,1:T(8,128)(2,1)} async-done(((bf16[16,8,5,256]{3,0,2,1:T(8,128)(2,1)}), bf16[256,8,5,256]{3,0,2,1:T(8,128)(2,1)}) %all-gather.8.cloned.1.call-update) | async-done | bytes 5242896 | tf_op jit(solution)/shard_map/all_gather | solution.py:57
  140.0 5.1 %multiply_convert_fusion = (bf16[128,8,256]{2,0,1:T(8,128)(2,1)S(1)}, bf16[128,8,256]{2,0,1:T(8,128)(2,1)}) fusion(f32[128,8,256]{2,1,0:T(8,128)} %bitcast.108, bf16[128,8,5,256]{3,0,2,1:T(8,128)(2,1)S(1)} %bitcast.99, bf16[256,8,5,256]{3,0,2,1:T(8,128)(2,1)} %all-gather.8.cloned.1.call-done), kind=kOutput, calls=%fused_computation.76 | convolution fusion | flops 676593664 | bytes 9961472 | tf_op jit(solution)/shard_map/tckb,bcke->tce/dot_general | solution.py:78
  151.5 3.4 %collective-permute-start.10 = (bf16[1,1,64,2048]{3,2,1,0:T(8,128)(2,1)S(1)}, bf16[1,1,64,2048]{3,2,1,0:T(8,128)(2,1)S(1)}, u32[]{:S(2)}, u32[]{:S(2)}) collective-permute-start(bf16[1,1,64,2048]{3,2,1,0:T(8,128)(2,1)S(1)} %get-tuple-element.31), channel_id=1, source_target_pairs={{8,0},{16,8},{24,16},{32,24},{40,32},{48,40},{56,48},{64,56},{72,6... | collective-permute-start | bytes 786440 | tf_op jit(solution)/shard_map/ppermute | solution.py:40
  154.9 2.7 convolution_bitcast_fusion.1
  162.3 5.7 %fusion = bf16[256,2,8,5,256]{0,4,3,2,1:T(8,128)(2,1)} fusion(f32[256,1,8,5,256]{0,4,3,2,1:T(8,128)S(1)} %convolution_bitcast_fusion, f32[256,1,8,5,256]{0,4,3,2,1:T(8,128)S(1)} %convolution_bitcast_fusion.1), kind=kLoop, calls=%fused_computation.3 | loop fusion | flops 15728640 | bytes 31457280 | tf_op jit(solution)/shard_map/convert_element_type | solution.py:130
  167.9 15.4 %copy.55 = bf16[256,2,8,5,256]{4,2,3,1,0:T(8,128)(2,1)} copy(bf16[256,2,8,5,256]{0,4,3,2,1:T(8,128)(2,1)} %fusion) | data formatting | bytes 20971520 | tf_op jit(solution)/shard_map/convert_element_type | solution.py:130
  184.4 4.3 %convolution_bitcast_fusion.2 = f32[128,8,5,256]{3,0,2,1:T(8,128)S(1)} fusion(bf16[256,8,5,256]{3,0,2,1:T(8,128)(2,1)} %all-gather.8.cloned.1.call-done, bf16[128,8,256]{2,0,1:T(8,128)(2,1)S(1)} %copy-done.4), kind=kOutput, calls=%fused_computation.19 | convolution fusion | flops 671088640 | bytes 11010048 | tf_op jit(solution)/shard_map/tce,bcke->tckb/dot_general | solution.py:111
  188.7 5.9 %fusion.5 = bf16[128,16,256]{2,1,0:T(8,128)(2,1)} fusion(f32[128,8,5,256]{3,0,2,1:T(8,128)S(1)} %convolution_bitcast_fusion.2, s32[8,5]{0,1:T(8,128)S(1)} %copy.43), kind=kOutput, calls=%fused_computation.35 | convolution fusion | flops 252183168 | bytes 6291616 | tf_op jit(solution)/shard_map/tckb,ckr->trb/dot_general | solution.py:117
  198.1 117.1 %psum.7 = bf16[9,2048]{1,0:T(8,128)(2,1)S(1)} all-reduce(bf16[9,2048]{1,0:T(8,128)(2,1)S(1)} %multiply_convert_fusion.1), channel_id=1, replica_groups=mesh['crop'=2,'rows'=16,'hid'=8] {'crop','rows'}, use_global_device_ids=true, to_apply=%region_11.13 | all-reduce | flops 18432 | bytes 73728 | tf_op jit(solution)/shard_map/psum | solution.py:110
  317.8 17.4 %reduce-scatter.3.cloned.1.call-done = bf16[1,2,64,512]{3,2,1,0:T(8,128)(2,1)} async-done(((bf16[1,2,64,4096]{3,2,1,0:T(8,128)(2,1)}), bf16[1,2,64,512]{3,2,1,0:T(8,128)(2,1)}) %reduce-scatter.3.cloned.1.call-update) | async-done | bytes 131088 | tf_op jit(solution)/shard_map/reduce_scatter | solution.py:120
  (81 shorter events, 36.8 us)
Async XLA Ops:
  7.2 11.4 %copy-start.5 = (bf16[1,2,64,512]{3,2,1,0:T(8,128)(2,1)S(1)}, bf16[1,2,64,512]{3,2,1,0:T(8,128)(2,1)}, u32[]{:S(2)}) copy-start(bf16[1,2,64,512]{3,2,1,0:T(8,128)(2,1)} %param.8) | copy-start | bytes 393220
  7.2 45.1 %all-gather.4.cloned.1.call-start = ((), (), s32[]{:S(2)}) async-start(), calls=%async_computation.2 | async-start | bytes 1179648 | tf_op jit(solution)/shard_map/all_gather | solution.py:62
  7.9 85.6 %all-gather.6.cloned.1.call-start = ((), (), s32[]{:S(2)}) async-start(), calls=%async_computation.3 | async-start | bytes 5570560 | tf_op jit(solution)/shard_map/all_gather | solution.py:58
  9.7 130.2 %all-gather.8.cloned.1.call-start = ((), (), s32[]{:S(2)}) async-start(), calls=%async_computation.4 | async-start | bytes 5570560 | tf_op jit(solution)/shard_map/all_gather | solution.py:57
  11.6 304.3 %reduce-scatter.5.cloned.1.call-start = ((), (), s32[]{:S(2)}) async-start(), calls=%async_computation.6 | async-start | bytes 10813440 | tf_op jit(solution)/shard_map/reduce_scatter | solution.py:129
  11.6 9.0 %collective-permute-start.3 = (bf16[1,2,64,512]{3,2,1,0:T(8,128)(2,1)}, bf16[1,2,64,512]{3,2,1,0:T(8,128)(2,1)S(1)}, u32[]{:S(2)}, u32[]{:S(2)}) collective-permute-start(bf16[1,2,64,512]{3,2,1,0:T(8,128)(2,1)} %param.8), channel_id=1, source_target_pairs={{0,7},{1,0},{2,1},{3,2},{4,3},{5,4},{6,5},{7,6},{8,15},{9,8},{10,9... | collective-permute-start | bytes 393224 | tf_op jit(solution)/shard_map/ppermute | solution.py:25
  17.6 6.7 %collective-permute-start.2 = (bf16[1,2,64,512]{3,2,1,0:T(8,128)(2,1)}, bf16[1,2,64,512]{3,2,1,0:T(8,128)(2,1)S(1)}, u32[]{:S(2)}, u32[]{:S(2)}) collective-permute-start(bf16[1,2,64,512]{3,2,1,0:T(8,128)(2,1)} %param.8), channel_id=1, source_target_pairs={{0,1},{1,2},{2,3},{3,4},{4,5},{5,6},{6,7},{7,0},{8,9},{9,10},{10,1... | collective-permute-start | bytes 393224 | tf_op jit(solution)/shard_map/ppermute | solution.py:20
  20.6 6.9 %collective-permute-start.5 = (bf16[1,2,64,512]{3,2,1,0:T(8,128)(2,1)S(1)}, bf16[1,2,64,512]{3,2,1,0:T(8,128)(2,1)S(1)}, u32[]{:S(2)}, u32[]{:S(2)}) collective-permute-start(bf16[1,2,64,512]{3,2,1,0:T(8,128)(2,1)S(1)} %collective-permute-done.3), channel_id=1, source_target_pairs={{0,7},{1,0},{2,1},{3,2},{4,3},{5,4},{6,5},{7,6},{8,15},{9,8},{10,9... | collective-permute-start | bytes 393224 | tf_op jit(solution)/shard_map/ppermute | solution.py:25
  24.2 7.0 %collective-permute-start.4 = (bf16[1,2,64,512]{3,2,1,0:T(8,128)(2,1)S(1)}, bf16[1,2,64,512]{3,2,1,0:T(8,128)(2,1)S(1)}, u32[]{:S(2)}, u32[]{:S(2)}) collective-permute-start(bf16[1,2,64,512]{3,2,1,0:T(8,128)(2,1)S(1)} %collective-permute-done.2), channel_id=1, source_target_pairs={{0,1},{1,2},{2,3},{3,4},{4,5},{5,6},{6,7},{7,0},{8,9},{9,10},{10,1... | collective-permute-start | bytes 393224 | tf_op jit(solution)/shard_map/ppermute | solution.py:20
  27.5 11.0 %collective-permute-start.7 = (bf16[1,2,64,512]{3,2,1,0:T(8,128)(2,1)S(1)}, bf16[1,2,64,512]{3,2,1,0:T(8,128)(2,1)S(1)}, u32[]{:S(2)}, u32[]{:S(2)}) collective-permute-start(bf16[1,2,64,512]{3,2,1,0:T(8,128)(2,1)S(1)} %collective-permute-done.5), channel_id=1, source_target_pairs={{0,7},{1,0},{2,1},{3,2},{4,3},{5,4},{6,5},{7,6},{8,15},{9,8},{10,9... | collective-permute-start | bytes 393224 | tf_op jit(solution)/shard_map/ppermute | solution.py:25
  31.2 7.3 %collective-permute-start.6 = (bf16[1,2,64,512]{3,2,1,0:T(8,128)(2,1)S(1)}, bf16[1,2,64,512]{3,2,1,0:T(8,128)(2,1)S(1)}, u32[]{:S(2)}, u32[]{:S(2)}) collective-permute-start(bf16[1,2,64,512]{3,2,1,0:T(8,128)(2,1)S(1)} %collective-permute-done.4), channel_id=1, source_target_pairs={{0,1},{1,2},{2,3},{3,4},{4,5},{5,6},{6,7},{7,0},{8,9},{9,10},{10,1... | collective-permute-start | bytes 393224 | tf_op jit(solution)/shard_map/ppermute | solution.py:20
  38.5 7.2 %collective-permute-start.8 = (bf16[1,2,64,512]{3,2,1,0:T(8,128)(2,1)S(1)}, bf16[1,2,64,512]{3,2,1,0:T(8,128)(2,1)S(1)}, u32[]{:S(2)}, u32[]{:S(2)}) collective-permute-start(bf16[1,2,64,512]{3,2,1,0:T(8,128)(2,1)S(1)} %collective-permute-done.6), channel_id=1, source_target_pairs={{0,1},{1,2},{2,3},{3,4},{4,5},{5,6},{6,7},{7,0},{8,9},{9,10},{10,1... | collective-permute-start | bytes 393224 | tf_op jit(solution)/shard_map/ppermute | solution.py:20
  61.2 36.6 %copy-start = (bf16[40,128,256]{2,1,0:T(8,128)(2,1)}, bf16[40,128,256]{2,1,0:T(8,128)(2,1)S(1)}, u32[]{:S(2)}) copy-start(bf16[40,128,256]{2,1,0:T(8,128)(2,1)S(1)} %get-tuple-element.43) | copy-start | bytes 7864324
  97.8 8.2 %copy-start.6 = (f32[9,2048]{1,0:T(8,128)S(1)}, f32[9,2048]{1,0:T(8,128)}, u32[]{:S(2)}) copy-start(f32[9,2048]{1,0:T(8,128)} %param.12) | copy-start | bytes 221188
  100.3 7.7 %collective-permute-start = (bf16[1,1,64,2048]{3,2,1,0:T(8,128)(2,1)S(1)}, bf16[1,1,64,2048]{3,2,1,0:T(8,128)(2,1)S(1)}, u32[]{:S(2)}, u32[]{:S(2)}) collective-permute-start(bf16[1,1,64,2048]{3,2,1,0:T(8,128)(2,1)S(1)} %get-tuple-element.32), channel_id=1, source_target_pairs={{0,8},{8,16},{16,24},{24,32},{32,40},{40,48},{48,56},{56,64},{64,7... | collective-permute-start | bytes 786440 | tf_op jit(solution)/shard_map/ppermute | solution.py:39
  102.4 8.8 %collective-permute-start.1 = (bf16[1,1,64,2048]{3,2,1,0:T(8,128)(2,1)S(1)}, bf16[1,1,64,2048]{3,2,1,0:T(8,128)(2,1)S(1)}, u32[]{:S(2)}, u32[]{:S(2)}) collective-permute-start(bf16[1,1,64,2048]{3,2,1,0:T(8,128)(2,1)S(1)} %get-tuple-element.33), channel_id=1, source_target_pairs={{8,0},{16,8},{24,16},{32,24},{40,32},{48,40},{56,48},{64,56},{72,6... | collective-permute-start | bytes 786440 | tf_op jit(solution)/shard_map/ppermute | solution.py:40
  111.4 28.6 %copy-start.2 = (bf16[40,128,256]{2,1,0:T(8,128)(2,1)S(1)}, bf16[40,128,256]{2,1,0:T(8,128)(2,1)}, u32[]{:S(2)}) copy-start(bf16[40,128,256]{2,1,0:T(8,128)(2,1)} %get-tuple-element.44) | copy-start | bytes 7864324
  149.3 8.2 %collective-permute-start.9 = (bf16[1,1,64,2048]{3,2,1,0:T(8,128)(2,1)S(1)}, bf16[1,1,64,2048]{3,2,1,0:T(8,128)(2,1)S(1)}, u32[]{:S(2)}, u32[]{:S(2)}) collective-permute-start(bf16[1,1,64,2048]{3,2,1,0:T(8,128)(2,1)S(1)} %get-tuple-element.30), channel_id=1, source_target_pairs={{0,8},{8,16},{16,24},{24,32},{32,40},{40,48},{48,56},{56,64},{64,7... | collective-permute-start | bytes 786440 | tf_op jit(solution)/shard_map/ppermute | solution.py:39
  151.5 7.3 %collective-permute-start.10 = (bf16[1,1,64,2048]{3,2,1,0:T(8,128)(2,1)S(1)}, bf16[1,1,64,2048]{3,2,1,0:T(8,128)(2,1)S(1)}, u32[]{:S(2)}, u32[]{:S(2)}) collective-permute-start(bf16[1,1,64,2048]{3,2,1,0:T(8,128)(2,1)S(1)} %get-tuple-element.31), channel_id=1, source_target_pairs={{8,0},{16,8},{24,16},{32,24},{40,32},{48,40},{56,48},{64,56},{72,6... | collective-permute-start | bytes 786440 | tf_op jit(solution)/shard_map/ppermute | solution.py:40
  154.9 3.9 %copy-start.3 = (bf16[1,2,64,2048]{3,2,1,0:T(8,128)(2,1)S(1)}, bf16[1,2,64,2048]{3,2,1,0:T(8,128)(2,1)}, u32[]{:S(2)}) copy-start(bf16[1,2,64,2048]{3,2,1,0:T(8,128)(2,1)} %reshape.189) | copy-start | bytes 1572868
  159.0 1.7 copy-start.1
  183.3 0.7 copy-start.7
  183.3 1.1 copy-start.4
  183.3 151.9 %reduce-scatter.3.cloned.1.call-start = ((), (), s32[]{:S(2)}) async-start(), calls=%async_computation.5 | async-start | bytes 1179648 | tf_op jit(solution)/shard_map/reduce_scatter | solution.py:120
Sparse Core Ops, SparseCore 0:
  9.8 42.4 all-gather.3
  54.7 38.7 all-gather.5
  95.9 44.0 all-gather.7
  183.5 110.2 reduce-scatter.4
  296.8 38.3 reduce-scatter.2
